TPU v7x, 32 devices: a whole 2x2x4 slice. The times are simulated.
32 devices in a mesh: dp: 2 (over y), row: 4 (over z), col: 4 (over x, core).
Axes of the slice: x: 2, y: 2, z: 4, core: 2. Of those that a mesh axis runs over, the one named last changes fastest.
Arguments:
- inputs: bfloat16 [18464, 1024], P(('dp', 'row'), 'col'), may hold values from -30 to 30
- query_weight: bfloat16 [1024, 1024], P('row', 'col'), may hold values from -7 to 7
- key_weight: bfloat16 [1024, 1024], P('row', 'col'), may hold values from -7 to 7
- value_weight: bfloat16 [1024, 1024], P('row', 'col'), may hold values from -0.1875 to 0.1875
- query_bias: float32 [1024], P('col'), may hold values from -3 to 3
- value_bias: float32 [1024], P('col'), may hold values from -0.3 to 0.3
- out_weight: bfloat16 [1024, 1024], P('col', 'row'), may hold values from -1.5 to 1.5
- out_bias: float32 [1024], P('col'), may hold values from -3 to 3
- up_weight: bfloat16 [1024, 4096], P('row', 'col'), may hold values from -0.1875 to 0.1875
- up_bias: float32 [4096], P('col'), may hold values from -3 to 3
- down_weight: bfloat16 [4096, 1024], P('col', 'row'), may hold values from -0.09375 to 0.09375
- down_bias: float32 [1024], P('col'), may hold values from -3 to 3
- first_gain: float32 [1024], P('col'), may hold values from 0.1 to 1.9
- first_shift: float32 [1024], P('col'), may hold values from -2 to 2
- second_gain: float32 [1024], P('col'), may hold values from 0.1 to 1.9
- second_shift: float32 [1024], P('col'), may hold values from -2 to 2
- cotangent: bfloat16 [18464, 1024], P(('dp', 'row'), 'col'), may hold values from -6 to 6
Outputs:
- outputs: bfloat16 [18464, 1024], P(('dp', 'row'), 'col')
- input_grad: float32 [18464, 1024], P(('dp', 'row'), 'col')
- query_weight_grad: float32 [1024, 1024], P('row', 'col')
- key_weight_grad: float32 [1024, 1024], P('row', 'col')
- value_weight_grad: float32 [1024, 1024], P('row', 'col')
- query_bias_grad: float32 [1024], P('col')
- value_bias_grad: float32 [1024], P('col')
- out_weight_grad: float32 [1024, 1024], P('col', 'row')
- out_bias_grad: float32 [1024], P('col')
- up_weight_grad: float32 [1024, 4096], P('row', 'col')
- up_bias_grad: float32 [4096], P('col')
- down_weight_grad: float32 [4096, 1024], P('col', 'row')
- down_bias_grad: float32 [1024], P('col')
- first_gain_grad: float32 [1024], P('col')
- first_shift_grad: float32 [1024], P('col')
- second_gain_grad: float32 [1024], P('col')
- second_shift_grad: float32 [1024], P('col')
All inputs are finite; a program needn't handle non-finite values.
Results may differ from a plain program's by a relative error of at most 0.012.
The roundings to bfloat16 on the way count: a program that leaves them out, or rounds other values in their place, can miss the bound.
Values may be sent and summed in bfloat16 or wider, within the bound.
No kernel may reach another device: no remote copies, remote signals or barrier semaphores. Data moves between devices by JAX's collectives and lax.ppermute only.
A program may use at most 192 MiB of HBM per device.

v0:
```python
import jax
import jax.numpy as jnp
from jax import lax
from jax.sharding import PartitionSpec as P

D = 1024
HD = 64
SEQ = 577


def matmul(left_side, right_side):
    return jnp.dot(left_side, right_side, preferred_element_type=jnp.float32)


def matmul_tn(left_side, right_side):
    return lax.dot_general(
        left_side, right_side, (((0,), (0,)), ((), ())), preferred_element_type=jnp.float32
    )


def matmul_nt(left_side, right_side):
    return lax.dot_general(
        left_side, right_side, (((1,), (1,)), ((), ())), preferred_element_type=jnp.float32
    )


def feature_totals(first, second):
    return lax.psum(
        (jnp.sum(first, axis=1, keepdims=True), jnp.sum(second, axis=1, keepdims=True)), "col"
    )


def gather_normed(values):
    return lax.all_gather(values, "col", axis=1, tiled=True)


def gather_grads(values):
    return lax.all_gather(values, "col", axis=1, tiled=True)


def scatter_partial(values):
    return lax.psum_scatter(values, "col", scatter_dimension=1, tiled=True)


def norm_forward(inputs_rows, gain_vector, shift_vector):
    row_total, squares = feature_totals(inputs_rows, inputs_rows * inputs_rows)
    middle = row_total / D
    spread = squares / D - middle * middle
    scaled = lax.rsqrt(spread + 1e-06)
    centred = (inputs_rows - middle) * scaled
    return (centred * gain_vector + shift_vector, centred, scaled)


def norm_backward(upstream, gain_vector, centred, scaled):
    dcentred = upstream * gain_vector
    first, second = feature_totals(dcentred, dcentred * centred)
    return scaled * (dcentred - first / D - centred * second / D)


def attend_image(operands):
    query_rows, key_rows, value_rows = operands
    scores = (
        jnp.einsum("qhd,khd->hqk", query_rows, key_rows, preferred_element_type=jnp.float32) * 0.125
    )
    row_peak = jnp.max(scores, axis=-1, keepdims=True)
    exponent = jnp.exp(scores - row_peak)
    row_total = jnp.sum(exponent, axis=-1, keepdims=True)
    soft_weights = (exponent / row_total).astype(jnp.bfloat16)
    mixed_rows = jnp.einsum(
        "hqk,khd->qhd", soft_weights, value_rows, preferred_element_type=jnp.float32
    )
    return (mixed_rows.astype(jnp.bfloat16), row_peak + jnp.log(row_total))


def attend_back(operands):
    query_rows, key_rows, value_rows, grad_rows, logsum = operands
    scores = (
        jnp.einsum("qhd,khd->hqk", query_rows, key_rows, preferred_element_type=jnp.float32) * 0.125
    )
    soft_weights = jnp.exp(scores - logsum)
    dprobs = jnp.einsum("qhd,khd->hqk", grad_rows, value_rows, preferred_element_type=jnp.float32)
    dvalues = jnp.einsum(
        "hqk,qhd->khd",
        soft_weights.astype(jnp.bfloat16),
        grad_rows,
        preferred_element_type=jnp.float32,
    )
    row_dot = jnp.sum(soft_weights * dprobs, axis=-1, keepdims=True)
    dscores = (soft_weights * (dprobs - row_dot)).astype(jnp.bfloat16)
    dqueries = (
        jnp.einsum("hqk,khd->qhd", dscores, key_rows, preferred_element_type=jnp.float32) * 0.125
    )
    key_grads = (
        jnp.einsum("hqk,qhd->khd", dscores, query_rows, preferred_element_type=jnp.float32) * 0.125
    )
    return (
        dqueries.astype(jnp.bfloat16),
        key_grads.astype(jnp.bfloat16),
        dvalues.astype(jnp.bfloat16),
    )


def gelu_exact(values):
    return jax.nn.gelu(values, approximate=False)


def local(
    inputs,
    query_weight,
    key_weight,
    value_weight,
    query_bias,
    value_bias,
    out_weight,
    out_bias,
    up_weight,
    up_bias,
    down_weight,
    down_bias,
    first_gain,
    first_shift,
    second_gain,
    second_shift,
    cotangent,
):
    tokens_here = inputs.shape[0]
    feature_width = inputs.shape[1]
    images = tokens_here // SEQ
    heads_here = feature_width // HD
    head_shape = (images, SEQ, heads_here, HD)
    residual = inputs.astype(jnp.float32)
    query_full, key_full, value_full, out_full, up_full, down_full = (
        lax.all_gather(query_weight, "row", axis=0, tiled=True),
        lax.all_gather(key_weight, "row", axis=0, tiled=True),
        lax.all_gather(value_weight, "row", axis=0, tiled=True),
        lax.all_gather(out_weight, "row", axis=1, tiled=True),
        lax.all_gather(up_weight, "row", axis=0, tiled=True),
        lax.all_gather(down_weight, "row", axis=1, tiled=True),
    )
    normed_one, centred_one, scaled_one = norm_forward(residual, first_gain, first_shift)
    wide_one = gather_normed(normed_one.astype(jnp.bfloat16))
    queries = (matmul(wide_one, query_full) + query_bias).astype(jnp.bfloat16)
    key_rows = matmul(wide_one, key_full).astype(jnp.bfloat16)
    values = (matmul(wide_one, value_full) + value_bias).astype(jnp.bfloat16)
    query_heads = queries.reshape(head_shape)
    key_heads = key_rows.reshape(head_shape)
    value_heads = values.reshape(head_shape)
    attended, logsums = lax.map(attend_image, (query_heads, key_heads, value_heads))
    attended = attended.reshape(tokens_here, feature_width)
    branch_attn = (
        lax.psum_scatter(matmul(attended, out_full), "col", scatter_dimension=1, tiled=True)
        + out_bias
    )
    middle_sum = residual + branch_attn
    normed_two, centred_two, scaled_two = norm_forward(middle_sum, second_gain, second_shift)
    wide_two = gather_normed(normed_two.astype(jnp.bfloat16))
    up_values = matmul(wide_two, up_full) + up_bias
    gelu_value, gelu_back = jax.vjp(gelu_exact, up_values)
    hidden = gelu_value.astype(jnp.bfloat16)
    branch_mlp = (
        lax.psum_scatter(
            matmul(hidden, down_full).astype(jnp.bfloat16), "col", scatter_dimension=1, tiled=True
        ).astype(jnp.float32)
        + down_bias
    )
    outputs = (middle_sum + branch_mlp).astype(jnp.bfloat16)
    grad_top = cotangent.astype(jnp.float32)
    down_bias_grad = jnp.sum(grad_top, axis=0)
    wide_grad = gather_grads(cotangent)
    down_grad_full = matmul_tn(hidden, wide_grad)
    hidden_grad = matmul_nt(wide_grad, down_full)
    pre_grad = gelu_back(hidden_grad)[0].astype(jnp.bfloat16)
    up_bias_grad = jnp.sum(pre_grad.astype(jnp.float32), axis=0)
    up_grad_full = matmul_tn(wide_two, pre_grad)
    normed_grad_two = scatter_partial(matmul_nt(pre_grad, up_full))
    second_gain_grad = jnp.sum(normed_grad_two * centred_two, axis=0)
    second_shift_grad = jnp.sum(normed_grad_two, axis=0)
    middle_grad = grad_top + norm_backward(normed_grad_two, second_gain, centred_two, scaled_two)
    attn_grad = middle_grad.astype(jnp.bfloat16)
    out_bias_grad = jnp.sum(attn_grad.astype(jnp.float32), axis=0)
    wide_attn_grad = gather_grads(attn_grad)
    out_grad_full = matmul_tn(attended, wide_attn_grad)
    head_grad = matmul_nt(wide_attn_grad, out_full).astype(jnp.bfloat16)
    dqueries, key_grads, dvalues = lax.map(
        attend_back, (query_heads, key_heads, value_heads, head_grad.reshape(head_shape), logsums)
    )
    dqueries = dqueries.reshape(tokens_here, feature_width)
    key_grads = key_grads.reshape(tokens_here, feature_width)
    dvalues = dvalues.reshape(tokens_here, feature_width)
    query_bias_grad = jnp.sum(dqueries.astype(jnp.float32), axis=0)
    value_bias_grad = jnp.sum(dvalues.astype(jnp.float32), axis=0)
    query_grad_full = matmul_tn(wide_one, dqueries)
    key_grad_full = matmul_tn(wide_one, key_grads)
    value_grad_full = matmul_tn(wide_one, dvalues)
    partial_one = (
        matmul_nt(dqueries, query_full)
        + matmul_nt(key_grads, key_full)
        + matmul_nt(dvalues, value_full)
    )
    normed_grad_one = scatter_partial(partial_one)
    first_gain_grad = jnp.sum(normed_grad_one * centred_one, axis=0)
    first_shift_grad = jnp.sum(normed_grad_one, axis=0)
    input_grad = middle_grad + norm_backward(normed_grad_one, first_gain, centred_one, scaled_one)
    vectors = jnp.concatenate(
        [
            query_bias_grad,
            value_bias_grad,
            out_bias_grad,
            down_bias_grad,
            first_gain_grad,
            first_shift_grad,
            second_gain_grad,
            second_shift_grad,
            up_bias_grad,
        ]
    )
    summed = lax.psum(
        (
            query_grad_full,
            key_grad_full,
            value_grad_full,
            out_grad_full,
            up_grad_full,
            down_grad_full,
            vectors,
        ),
        ("dp", "row"),
    )
    row_index = lax.axis_index("row")
    query_grad = lax.dynamic_slice_in_dim(
        summed[0], row_index * query_weight.shape[0], query_weight.shape[0], 0
    )
    key_grad = lax.dynamic_slice_in_dim(
        summed[1], row_index * key_weight.shape[0], key_weight.shape[0], 0
    )
    value_grad = lax.dynamic_slice_in_dim(
        summed[2], row_index * value_weight.shape[0], value_weight.shape[0], 0
    )
    out_grad = lax.dynamic_slice_in_dim(
        summed[3], row_index * out_weight.shape[1], out_weight.shape[1], 1
    )
    up_grad = lax.dynamic_slice_in_dim(
        summed[4], row_index * up_weight.shape[0], up_weight.shape[0], 0
    )
    down_grad = lax.dynamic_slice_in_dim(
        summed[5], row_index * down_weight.shape[1], down_weight.shape[1], 1
    )
    vector_sums = summed[6]
    pieces = [
        vector_sums[feature_width * place : feature_width * (place + 1)] for place in range(8)
    ]
    up_bias_sum = vector_sums[8 * feature_width :]
    return (
        outputs,
        input_grad,
        query_grad,
        key_grad,
        value_grad,
        pieces[0],
        pieces[1],
        out_grad,
        pieces[2],
        up_grad,
        up_bias_sum,
        down_grad,
        pieces[3],
        pieces[4],
        pieces[5],
        pieces[6],
        pieces[7],
    )


def solution(mesh):
    in_specs = (
        P(("dp", "row"), "col"),
        P("row", "col"),
        P("row", "col"),
        P("row", "col"),
        P("col"),
        P("col"),
        P("col", "row"),
        P("col"),
        P("row", "col"),
        P("col"),
        P("col", "row"),
        P("col"),
        P("col"),
        P("col"),
        P("col"),
        P("col"),
        P(("dp", "row"), "col"),
    )
    out_specs = (
        P(("dp", "row"), "col"),
        P(("dp", "row"), "col"),
        P("row", "col"),
        P("row", "col"),
        P("row", "col"),
        P("col"),
        P("col"),
        P("col", "row"),
        P("col"),
        P("row", "col"),
        P("col"),
        P("col", "row"),
        P("col"),
        P("col"),
        P("col"),
        P("col"),
        P("col"),
    )
    return jax.shard_map(local, mesh=mesh, in_specs=in_specs, out_specs=out_specs, check_vma=False)
```

profile of v0, /device:TPU:0, one launch (start us, length us, event | category | flops | bytes accessed | tf_op | source)
XLA Modules:
  0.0 1243.2 jit_solution(17970794028962596964)
XLA Ops:
  10.2 12.9 %all-reduce.4 = (f32[2308,1]{0,1:T(1,128)S(1)}, f32[2308,1]{0,1:T(1,128)S(1)}) all-reduce(f32[2308,1]{0,1:T(1,128)S(1)} %broadcast_in_dim.57, f32[2308,1]{0,1:T(1,128)S(1)} %broadcast_in_dim.58), channel_id=1, replica_groups=mesh['dp'=2,'row'=4,'col'=4] {'col'}, use_global_device_ids=true, to_apply=%region_1.0 | all-reduce | flops 4616 | bytes 36928 | tf_op jit(solution)/shard_map/psum | solution.py:28
  27.2 15.0 %all_gather.31 = bf16[1024,256]{1,0:T(8,128)(2,1)S(1)} all-gather(bf16[256,256]{1,0:T(8,128)(2,1)S(1)} %copy-done.27), channel_id=1, replica_groups=mesh['dp'=2,'row'=4,'col'=4] {'row'}, dimensions={0}, use_global_device_ids=true | all-gather | bytes 655360 | tf_op jit(solution)/shard_map/all_gather | solution.py:135
  42.2 17.4 %all_gather.32 = bf16[1024,256]{1,0:T(8,128)(2,1)S(1)} all-gather(bf16[256,256]{1,0:T(8,128)(2,1)S(1)} %copy-done.28), channel_id=1, replica_groups=mesh['dp'=2,'row'=4,'col'=4] {'row'}, dimensions={0}, use_global_device_ids=true | all-gather | bytes 655360 | tf_op jit(solution)/shard_map/all_gather | solution.py:133
  59.7 14.8 %all_gather.33 = bf16[1024,256]{1,0:T(8,128)(2,1)S(1)} all-gather(bf16[256,256]{1,0:T(8,128)(2,1)S(1)} %copy-done.29), channel_id=1, replica_groups=mesh['dp'=2,'row'=4,'col'=4] {'row'}, dimensions={0}, use_global_device_ids=true | all-gather | bytes 655360 | tf_op jit(solution)/shard_map/all_gather | solution.py:134
  74.5 15.8 %all_gather.34 = bf16[256,1024]{1,0:T(8,128)(2,1)} all-gather(bf16[256,256]{1,0:T(8,128)(2,1)S(1)} %copy-done.30), channel_id=1, replica_groups=mesh['dp'=2,'row'=4,'col'=4] {'row'}, dimensions={1}, use_global_device_ids=true | all-gather | bytes 655360 | tf_op jit(solution)/shard_map/all_gather | solution.py:136
  121.4 23.7 %while.26 = (s32[]{:T(128)}, bf16[4,577,4,64]{1,3,2,0:T(8,128)(2,1)}, f32[4,4,577,1]{2,1,3,0:T(4,128)}, bf16[4,577,4,64]{1,3,2,0:T(8,128)(2,1)}, bf16[4,577,4,64...) while((s32[]{:T(128)}, bf16[4,577,4,64]{1,3,2,0:T(8,128)(2,1)}, ...), condition=%wide.region_7.8_spmd, body=%wide.region_4.7_spmd.sunk | while | flops 353050112 | bytes 17368812 | solution.py:148
  149.5 14.1 %reshape.96 = bf16[2308,256]{0,1:T(8,128)(2,1)} reshape(bf16[4,577,4,64]{1,0,3,2:T(4,128)(2,1)} %copy.55) | data formatting | bytes 2363392 | tf_op jit(solution)/shard_map/reshape | solution.py:149
  163.7 6.3 fusion.82
  170.7 78.4 %reduce-scatter.5.cloned.1.call-done = f32[2308,256]{1,0:T(8,128)} async-done(((f32[2308,1024]{1,0:T(8,128)}), f32[2308,256]{1,0:T(8,128)}) %reduce-scatter.5.cloned.1.call-update) | async-done | bytes 2363408 | tf_op jit(solution)/shard_map/reduce_scatter | solution.py:151
  251.6 10.2 all-reduce.3
  266.8 37.3 %all-gather.9.cloned.1.call-done = bf16[2308,1024]{1,0:T(8,128)(2,1)} async-done(((bf16[2308,256]{1,0:T(8,128)(2,1)}), bf16[2308,1024]{1,0:T(8,128)(2,1)}) %all-gather.9.cloned.1.call-update) | async-done | bytes 4726800 | tf_op jit(solution)/shard_map/all_gather | solution.py:34
  304.0 10.1 fusion.83
  314.2 37.5 %all-gather.13.cloned.1.call-done = bf16[1024,1024]{1,0:T(8,128)(2,1)} async-done(((bf16[1024,256]{1,0:T(8,128)(2,1)}), bf16[1024,1024]{1,0:T(8,128)(2,1)}) %all-gather.13.cloned.1.call-update) | async-done | bytes 2097168 | tf_op jit(solution)/shard_map/all_gather | solution.py:138
  351.6 37.8 %all-gather.15.cloned.1.call-done = bf16[2308,1024]{1,0:T(8,128)(2,1)} async-done(((bf16[2308,256]{1,0:T(8,128)(2,1)}), bf16[2308,1024]{1,0:T(8,128)(2,1)}) %all-gather.15.cloned.1.call-update) | async-done | bytes 4726800 | tf_op jit(solution)/shard_map/all_gather | solution.py:38
  389.4 32.0 %convert_reduce_fusion = (f32[1024]{0:T(1024)}, bf16[2308,1024]{1,0:T(8,128)(2,1)S(1)}, f32[2308,1024]{1,0:T(8,128)}) fusion(f32[2308,1024]{1,0:T(8,128)} %fusion.83, f32[1024]{0:T(1024)S(1)} %copy-done.36, bf16[2308,1024]{1,0:T(8,128)(2,1)} %all-gather.15.cloned.1.call-done, bf16[1024,1024]{1,0:T(8,128)(2,1)} %all-gather.13.cloned.1.call-done), kind=kOutput, calls=%fused_computation.62 | convolution fusion | flops 5017480192 | bytes 30466048 | tf_op jit(solution)/shard_map/dot_general | solution.py:22
  423.6 8.0 fusion.84
  432.1 13.0 %multiply_convert_fusion.1 = bf16[2308,1024]{1,0:T(8,128)(2,1)} fusion(f32[2308,1024]{1,0:T(8,128)} %get-tuple-element.196, f32[2308,1024]{1,0:T(8,128)} %fusion.83, f32[1024]{0:T(1024)S(1)} %copy-done.36), kind=kLoop, calls=%fused_computation.65 | loop fusion | flops 9453568 | bytes 23638016 | tf_op jit(solution)/shard_map/convert_element_type | solution.py:159
  445.1 10.0 convolution_convert_fusion
  455.2 54.5 %reduce-scatter.9.cloned.1.call-done = f32[2308,256]{1,0:T(8,128)} async-done(((f32[2308,1024]{1,0:T(8,128)}), f32[2308,256]{1,0:T(8,128)}) %reduce-scatter.9.cloned.1.call-update) | async-done | bytes 2363408 | tf_op jit(solution)/shard_map/reduce_scatter | solution.py:42
  513.9 11.4 all-reduce.2
  526.7 33.3 %reduce-scatter.7.cloned.1.call-done = bf16[2308,256]{1,0:T(8,128)(2,1)} async-done(((bf16[2308,1024]{1,0:T(8,128)(2,1)}), bf16[2308,256]{1,0:T(8,128)(2,1)}) %reduce-scatter.7.cloned.1.call-update) | async-done | bytes 1181712 | tf_op jit(solution)/shard_map/reduce_scatter | solution.py:161
  560.1 6.5 convert_reduce_fusion.5
  566.6 10.4 fusion.91
  577.1 8.9 fusion.92
  586.0 18.8 %all-gather.17.cloned.1.call-done = bf16[2308,1024]{1,0:T(8,128)(2,1)} async-done(((bf16[2308,256]{1,0:T(8,128)(2,1)}), bf16[2308,1024]{1,0:T(8,128)(2,1)}) %all-gather.17.cloned.1.call-update) | async-done | bytes 4726800 | tf_op jit(solution)/shard_map/all_gather | solution.py:38
  619.2 43.5 %while.27 = (s32[]{:T(128)}, bf16[4,577,4,64]{1,3,2,0:T(8,128)(2,1)}, bf16[4,577,4,64]{1,3,2,0:T(8,128)(2,1)}, bf16[4,577,4,64]{1,3,2,0:T(8,128)(2,1)}, bf16[4,5...) while((s32[]{:T(128)}, ...), condition=%wide.region_21.22_spmd, body=%wide.region_19.21_spmd.sunk | while | flops 869015040 | bytes 49986844 | solution.py:184
  682.1 5.2 fusion.87
  697.5 5.1 add_add_fusion
  709.8 378.3 %all-reduce.7.cloned.1.call-done = (f32[1024,256]{1,0:T(8,128)}, f32[1024,256]{1,0:T(8,128)}, f32[1024,256]{1,0:T(8,128)}, f32[256,1024]{1,0:T(8,128)}, f32[1024,1024]{1,0:T(8,128)}, /*index=5*/f32[1024,1024]{1,0:T(8,128)}) async-done(((f32[1024,256]{1,0:T(8,128)}, f32[1024,256]{1,0:T(8,128)}, f32[1024,256]{1,0:T(8,128)}, f32[256,1024]{1,0:T(8,128)}, f32[1024,1024]{1,0:T(8,128)}, ...) | async-done | bytes 12582928 | tf_op jit(solution)/shard_map/psum | solution.py:217
  1097.0 70.7 %reduce-scatter.11.cloned.1.call-done = f32[2308,256]{1,0:T(8,128)} async-done(((f32[2308,1024]{1,0:T(8,128)}), f32[2308,256]{1,0:T(8,128)}) %reduce-scatter.11.cloned.1.call-update) | async-done | bytes 2363408 | tf_op jit(solution)/shard_map/reduce_scatter | solution.py:42
  1177.2 37.3 %psum.116 = f32[3072]{0:T(1024)} all-reduce(f32[3072]{0:T(1024)} %constant_dynamic-update-slice_fusion), channel_id=1, replica_groups=mesh['dp'=2,'row'=4,'col'=4] {'dp','row'}, use_global_device_ids=true, to_apply=%region_39.40 | all-reduce | flops 3072 | bytes 24576 | tf_op jit(solution)/shard_map/psum | solution.py:217
  1218.4 11.6 all-reduce.1
  (231 shorter events, 203.9 us)
Async XLA Ops:
  8.0 19.1 %copy-start.27 = (bf16[256,256]{1,0:T(8,128)(2,1)S(1)}, bf16[256,256]{1,0:T(8,128)(2,1)}, u32[]{:S(2)}) copy-start(bf16[256,256]{1,0:T(8,128)(2,1)} %param.24) | copy-start | bytes 393220
  8.0 34.2 %copy-start.28 = (bf16[256,256]{1,0:T(8,128)(2,1)S(1)}, bf16[256,256]{1,0:T(8,128)(2,1)}, u32[]{:S(2)}) copy-start(bf16[256,256]{1,0:T(8,128)(2,1)} %param.22) | copy-start | bytes 393220
  8.0 51.6 %copy-start.29 = (bf16[256,256]{1,0:T(8,128)(2,1)S(1)}, bf16[256,256]{1,0:T(8,128)(2,1)}, u32[]{:S(2)}) copy-start(bf16[256,256]{1,0:T(8,128)(2,1)} %param.23) | copy-start | bytes 393220
  8.1 82.2 %all-gather.7.cloned.1.call-start = ((), (), s32[]{:S(2)}) async-start(), calls=%async_computation.4 | async-start | bytes 5918720 | tf_op jit(solution)/shard_map/all_gather | solution.py:34
  10.2 64.3 %copy-start.30 = (bf16[256,256]{1,0:T(8,128)(2,1)S(1)}, bf16[256,256]{1,0:T(8,128)(2,1)}, u32[]{:S(2)}) copy-start(bf16[256,256]{1,0:T(8,128)(2,1)} %param.27) | copy-start | bytes 393220
  23.9 66.4 %copy-start.38 = (f32[256]{0:T(256)S(1)}, f32[256]{0:T(256)}, u32[]{:S(2)}) copy-start(f32[256]{0:T(256)} %param.26) | copy-start | bytes 3076
  27.1 222.0 %reduce-scatter.5.cloned.1.call-start = ((), (), s32[]{:S(2)}) async-start(), calls=%async_computation.5 | async-start | bytes 11837440 | tf_op jit(solution)/shard_map/reduce_scatter | solution.py:151
  42.2 48.0 %copy-start.16 = (bf16[1024,256]{1,0:T(8,128)(2,1)}, bf16[1024,256]{1,0:T(8,128)(2,1)S(1)}, u32[]{:S(2)}) copy-start(bf16[1024,256]{1,0:T(8,128)(2,1)S(1)} %all_gather.31) | copy-start | bytes 1572868
  59.7 41.9 %copy-start.18 = (bf16[1024,256]{1,0:T(8,128)(2,1)}, bf16[1024,256]{1,0:T(8,128)(2,1)S(1)}, u32[]{:S(2)}) copy-start(bf16[1024,256]{1,0:T(8,128)(2,1)S(1)} %all_gather.32) | copy-start | bytes 1572868
  74.5 36.4 %copy-start.20 = (bf16[1024,256]{1,0:T(8,128)(2,1)}, bf16[1024,256]{1,0:T(8,128)(2,1)S(1)}, u32[]{:S(2)}) copy-start(bf16[1024,256]{1,0:T(8,128)(2,1)S(1)} %all_gather.33) | copy-start | bytes 1572868
  145.2 24.9 %copy-start.2 = (bf16[4,577,4,64]{1,3,2,0:T(8,128)(2,1)}, bf16[4,577,4,64]{1,3,2,0:T(8,128)(2,1)S(1)}, u32[]{:S(2)}) copy-start(bf16[4,577,4,64]{1,3,2,0:T(8,128)(2,1)S(1)} %get-tuple-element.398) | copy-start | bytes 3545092
  145.2 24.9 %copy-start.4 = (bf16[4,577,4,64]{1,3,2,0:T(8,128)(2,1)}, bf16[4,577,4,64]{1,3,2,0:T(8,128)(2,1)S(1)}, u32[]{:S(2)}) copy-start(bf16[4,577,4,64]{1,3,2,0:T(8,128)(2,1)S(1)} %get-tuple-element.399) | copy-start | bytes 3545092
  145.2 18.5 %copy-start.21 = (bf16[256,1024]{1,0:T(8,128)(2,1)S(1)}, bf16[256,1024]{1,0:T(8,128)(2,1)}, u32[]{:S(2)}) copy-start(bf16[256,1024]{1,0:T(8,128)(2,1)} %all_gather.34) | copy-start | bytes 1572868
  170.0 79.1 %copy-start = (bf16[2308,256]{1,0:T(8,128)(2,1)S(1)}, bf16[2308,256]{1,0:T(8,128)(2,1)}, u32[]{:S(2)}) copy-start(bf16[2308,256]{1,0:T(8,128)(2,1)} %param.21) | copy-start | bytes 3545092
  170.1 96.7 %all-gather.11.cloned.1.call-start = ((), (), s32[]{:S(2)}) async-start(), calls=%async_computation.7 | async-start | bytes 2621440 | tf_op jit(solution)/shard_map/all_gather | solution.py:137
  170.6 91.9 %copy-start.32 = (f32[256]{0:T(256)S(1)}, f32[256]{0:T(256)}, u32[]{:S(2)}) copy-start(f32[256]{0:T(256)} %param.35) | copy-start | bytes 3076
  170.6 133.4 %all-gather.9.cloned.1.call-start = ((), (), s32[]{:S(2)}) async-start(), calls=%async_computation.6 | async-start | bytes 5918720 | tf_op jit(solution)/shard_map/all_gather | solution.py:34
  265.4 86.3 %all-gather.13.cloned.1.call-start = ((), (), s32[]{:S(2)}) async-start(), calls=%async_computation.8 | async-start | bytes 2621440 | tf_op jit(solution)/shard_map/all_gather | solution.py:138
  266.0 123.5 %all-gather.15.cloned.1.call-start = ((), (), s32[]{:S(2)}) async-start(), calls=%async_computation.10 | async-start | bytes 5918720 | tf_op jit(solution)/shard_map/all_gather | solution.py:38
  266.7 122.7 %copy-start.36 = (f32[1024]{0:T(1024)S(1)}, f32[1024]{0:T(1024)}, u32[]{:S(2)}) copy-start(f32[1024]{0:T(1024)} %param.30) | copy-start | bytes 12292
  266.7 243.0 %reduce-scatter.9.cloned.1.call-start = ((), (), s32[]{:S(2)}) async-start(), calls=%async_computation.11 | async-start | bytes 11837440 | tf_op jit(solution)/shard_map/reduce_scatter | solution.py:42
  389.4 34.2 %copy-start.37 = (bf16[1024,1024]{1,0:T(8,128)(2,1)S(1)}, bf16[1024,1024]{1,0:T(8,128)(2,1)}, u32[]{:S(2)}) copy-start(bf16[1024,1024]{1,0:T(8,128)(2,1)} %all-gather.11.cloned.1.call-done) | copy-start | bytes 6291460
  431.7 128.4 %reduce-scatter.7.cloned.1.call-start = ((), (), s32[]{:S(2)}) async-start(), calls=%async_computation.9 | async-start | bytes 5918720 | tf_op jit(solution)/shard_map/reduce_scatter | solution.py:161
  455.1 104.9 %copy-start.15 = (bf16[2308,256]{1,0:T(8,128)(2,1)S(1)}, bf16[2308,256]{1,0:T(8,128)(2,1)}, u32[]{:S(2)}) copy-start(bf16[2308,256]{1,0:T(8,128)(2,1)} %param.37) | copy-start | bytes 3545092
  455.2 149.7 %all-gather.17.cloned.1.call-start = ((), (), s32[]{:S(2)}) async-start(), calls=%async_computation.12 | async-start | bytes 5918720 | tf_op jit(solution)/shard_map/all_gather | solution.py:38
  566.6 10.5 slice-start
  566.6 521.6 %all-reduce.7.cloned.1.call-start = ((), (), s32[]{:S(2)}) async-start(), calls=%async_computation.14 | async-start | bytes 25165824 | tf_op jit(solution)/shard_map/psum | solution.py:217
  577.1 27.8 %copy-start.22 = (bf16[256,1024]{1,0:T(8,128)(2,1)S(1)}, bf16[256,1024]{1,0:T(8,128)(2,1)}, u32[]{:S(2)}) copy-start(bf16[256,1024]{1,0:T(8,128)(2,1)} %all_gather.34) | copy-start | bytes 1572868
  693.0 474.7 %reduce-scatter.11.cloned.1.call-start = ((), (), s32[]{:S(2)}) async-start(), calls=%async_computation.13 | async-start | bytes 11837440 | tf_op jit(solution)/shard_map/reduce_scatter | solution.py:42
  1088.2 79.5 %copy-start.1 = (bf16[2308,256]{1,0:T(8,128)(2,1)S(1)}, bf16[2308,256]{1,0:T(8,128)(2,1)}, u32[]{:S(2)}) copy-start(bf16[2308,256]{1,0:T(8,128)(2,1)} %param.21) | copy-start | bytes 3545092
  1088.2 79.5 %copy-start.31 = (f32[256]{0:T(256)S(1)}, f32[256]{0:T(256)}, u32[]{:S(2)}) copy-start(f32[256]{0:T(256)} %param.33) | copy-start | bytes 3076
  1094.2 136.6 %copy-start.8 = (f32[2308,256]{1,0:T(8,128)S(1)}, f32[2308,256]{1,0:T(8,128)}, u32[]{:S(2)}) copy-start(f32[2308,256]{1,0:T(8,128)} %get-tuple-element.199) | copy-start | bytes 7090180
  (27 other events, 113.4 us)
Sparse Core Ops, SparseCore 0:
  27.2 38.4 all-gather.6
  170.2 78.9 reduce-scatter.4
  566.7 38.1 all-gather.16
  693.1 395.0 all-reduce.6
  1090.6 77.0 reduce-scatter.10
Sparse Core Ops, SparseCore 1:
  172.1 46.4 all-gather.10
  265.5 38.5 all-gather.8
  305.5 46.1 all-gather.12
  353.2 36.2 all-gather.14
  431.8 77.8 reduce-scatter.8
  512.2 47.8 reduce-scatter.6
where the time goes:
time: 1250 us; the launch traced here: 1240 us
  waiting for transfers between devices  749 us (60%)
  matrix products  179 us (14%)
  blocking collectives  147 us (12%)
  local copies, waits for them, and re-layouts  93.2 us (7%)
  other arithmetic  58.6 us (5%)
  between operations  16.1 us (1%)
    psum x1, waiting for transfers between devices, local(): lax.psum((query_grad_full, key_grad_full, value_grad_full, out_grad_full,...  378 us
    reduce_scatter x2, waiting for transfers between devices, scatter_partial(): return lax.psum_scatter(values, 'col', scatter_dimension=1, tiled=True)  125 us
    reduce_scatter x1, waiting for transfers between devices, local(): lax.psum_scatter(matmul(attended, out_full), 'col', scatter_dimension=1,...  78.4 us
    all_gather x2, waiting for transfers between devices, gather_grads(): return lax.all_gather(values, 'col', axis=1, tiled=True)  56.6 us
    dot_general x6, matrix products, matmul_nt(): lax.dot_general(left_side, right_side, (((1,), (1,)), ((), ())), preferre...  53.1 us
    psum x4, blocking collectives, feature_totals(): lax.psum((jnp.sum(first, axis=1, keepdims=True), jnp.sum(second, axis=1,...  46.3 us
    dot_general x6, matrix products, matmul(): return jnp.dot(left_side, right_side, preferred_element_type=jnp.float32)  38.7 us
    all_gather x1, waiting for transfers between devices, local(): lax.all_gather(down_weight, 'row', axis=1, tiled=True)  37.5 us
  transfers between devices with their start and end apart: 11, of which 9 were waited for; matrix products, arithmetic and copies ran while one was open for 7% of the time, Pallas kernels for 0%

commit v1 on v0

--- a/solution.py
+++ b/solution.py
@@ -215,16 +215,19 @@
         ]
     )
     summed = lax.psum(
-        (
-            query_grad_full,
-            key_grad_full,
-            value_grad_full,
-            out_grad_full,
-            up_grad_full,
-            down_grad_full,
-            vectors,
+        lax.psum(
+            (
+                query_grad_full,
+                key_grad_full,
+                value_grad_full,
+                out_grad_full,
+                up_grad_full,
+                down_grad_full,
+                vectors,
+            ),
+            "row",
         ),
-        ("dp", "row"),
+        "dp",
     )
     row_index = lax.axis_index("row")
     query_grad = lax.dynamic_slice_in_dim(

time: 1250 us -> 1420 us (1.14)
  waiting for transfers between devices: 749 us -> 932 us
    psum x0 -> x1, waiting for transfers between devices: none -> 218 us  [local(): lax.psum(lax.psum((query_grad_full, key_grad_full, value_grad_full, out_g...]
    reduce_scatter x2, waiting for transfers between devices: 125 us -> 54.5 us  [scatter_partial(): return lax.psum_scatter(values, 'col', scatter_dimension=1, tiled=True)]
    psum x1, waiting for transfers between devices: 378 us -> 415 us  [local(): lax.psum((query_grad_full, key_grad_full, value_grad_full, out_grad_full,...]
    psum x1, blocking collectives: 37.3 us -> 17.6 us  [local(): lax.psum((query_grad_full, key_grad_full, value_grad_full, out_grad_full,...]
  transfers between devices with their start and end apart: 11 -> 12, of which waited for: 9 -> 9; matrix products, arithmetic and copies ran while one was open for 7% -> 7% of each run, Pallas kernels for 0% -> 0%
where the time goes in v1:
time: 1420 us
  waiting for transfers between devices  932 us (66%)
  matrix products  177 us (12%)
  blocking collectives  138 us (10%)
  local copies, waits for them, and re-layouts  91.6 us (6%)
  other arithmetic  59.4 us (4%)
  between operations  16.1 us (1%)
    psum x1, waiting for transfers between devices, local(): lax.psum((query_grad_full, key_grad_full, value_grad_full, out_grad_full,...  415 us
    psum x1, waiting for transfers between devices, local(): lax.psum(lax.psum((query_grad_full, key_grad_full, value_grad_full, out_g...  218 us
    reduce_scatter x1, waiting for transfers between devices, local(): lax.psum_scatter(matmul(attended, out_full), 'col', scatter_dimension=1,...  78.4 us
    all_gather x2, waiting for transfers between devices, gather_grads(): return lax.all_gather(values, 'col', axis=1, tiled=True)  56.6 us
    reduce_scatter x2, waiting for transfers between devices, scatter_partial(): return lax.psum_scatter(values, 'col', scatter_dimension=1, tiled=True)  54.5 us
    dot_general x6, matrix products, matmul_nt(): lax.dot_general(left_side, right_side, (((1,), (1,)), ((), ())), preferre...  53.3 us
    psum x4, blocking collectives, feature_totals(): lax.psum((jnp.sum(first, axis=1, keepdims=True), jnp.sum(second, axis=1,...  46.8 us
    dot_general x6, matrix products, matmul(): return jnp.dot(left_side, right_side, preferred_element_type=jnp.float32)  38.8 us
  transfers between devices with their start and end apart: 12, of which 9 were waited for; matrix products, arithmetic and copies ran while one was open for 7% of the time, Pallas kernels for 0%

profile of v1, /device:TPU:0, one launch (start us, length us, event | category | flops | bytes accessed | tf_op | source)
XLA Modules:
  0.0 1415.3 jit_solution(9197477079363353562)
XLA Ops:
  10.2 12.9 all-reduce.3
  27.2 15.0 %all_gather.31 = bf16[1024,256]{1,0:T(8,128)(2,1)S(1)} all-gather(bf16[256,256]{1,0:T(8,128)(2,1)S(1)} %copy-done.27), channel_id=1, replica_groups=mesh['dp'=2,'row'=4,'col'=4] {'row'}, dimensions={0}, use_global_device_ids=true | all-gather | bytes 655360 | tf_op jit(solution)/shard_map/all_gather | solution.py:135
  42.2 17.4 %all_gather.32 = bf16[1024,256]{1,0:T(8,128)(2,1)S(1)} all-gather(bf16[256,256]{1,0:T(8,128)(2,1)S(1)} %copy-done.28), channel_id=1, replica_groups=mesh['dp'=2,'row'=4,'col'=4] {'row'}, dimensions={0}, use_global_device_ids=true | all-gather | bytes 655360 | tf_op jit(solution)/shard_map/all_gather | solution.py:133
  59.7 14.8 %all_gather.33 = bf16[1024,256]{1,0:T(8,128)(2,1)S(1)} all-gather(bf16[256,256]{1,0:T(8,128)(2,1)S(1)} %copy-done.29), channel_id=1, replica_groups=mesh['dp'=2,'row'=4,'col'=4] {'row'}, dimensions={0}, use_global_device_ids=true | all-gather | bytes 655360 | tf_op jit(solution)/shard_map/all_gather | solution.py:134
  74.5 15.8 %all_gather.34 = bf16[256,1024]{1,0:T(8,128)(2,1)} all-gather(bf16[256,256]{1,0:T(8,128)(2,1)S(1)} %copy-done.30), channel_id=1, replica_groups=mesh['dp'=2,'row'=4,'col'=4] {'row'}, dimensions={1}, use_global_device_ids=true | all-gather | bytes 655360 | tf_op jit(solution)/shard_map/all_gather | solution.py:136
  121.6 23.7 %while.26 = (s32[]{:T(128)}, bf16[4,577,4,64]{1,3,2,0:T(8,128)(2,1)}, f32[4,4,577,1]{2,1,3,0:T(4,128)}, bf16[4,577,4,64]{1,3,2,0:T(8,128)(2,1)}, bf16[4,577,4,64...) while((s32[]{:T(128)}, bf16[4,577,4,64]{1,3,2,0:T(8,128)(2,1)}, ...), condition=%wide.region_7.8_spmd, body=%wide.region_4.7_spmd.sunk | while | flops 353050112 | bytes 17368812 | solution.py:148
  153.4 6.3 fusion.82
  160.4 78.4 %reduce-scatter.5.cloned.1.call-done = f32[2308,256]{1,0:T(8,128)} async-done(((f32[2308,1024]{1,0:T(8,128)}), f32[2308,256]{1,0:T(8,128)}) %reduce-scatter.5.cloned.1.call-update) | async-done | bytes 2363408 | tf_op jit(solution)/shard_map/reduce_scatter | solution.py:151
  241.3 10.2 all-reduce.2
  256.5 37.3 %all-gather.9.cloned.1.call-done = bf16[2308,1024]{1,0:T(8,128)(2,1)} async-done(((bf16[2308,256]{1,0:T(8,128)(2,1)}), bf16[2308,1024]{1,0:T(8,128)(2,1)}) %all-gather.9.cloned.1.call-update) | async-done | bytes 4726800 | tf_op jit(solution)/shard_map/all_gather | solution.py:34
  293.7 10.1 fusion.83
  303.8 37.5 %all-gather.13.cloned.1.call-done = bf16[1024,1024]{1,0:T(8,128)(2,1)} async-done(((bf16[1024,256]{1,0:T(8,128)(2,1)}), bf16[1024,1024]{1,0:T(8,128)(2,1)}) %all-gather.13.cloned.1.call-update) | async-done | bytes 2097168 | tf_op jit(solution)/shard_map/all_gather | solution.py:138
  341.3 37.8 %all-gather.15.cloned.1.call-done = bf16[2308,1024]{1,0:T(8,128)(2,1)} async-done(((bf16[2308,256]{1,0:T(8,128)(2,1)}), bf16[2308,1024]{1,0:T(8,128)(2,1)}) %all-gather.15.cloned.1.call-update) | async-done | bytes 4726800 | tf_op jit(solution)/shard_map/all_gather | solution.py:38
  379.1 32.0 %convert_reduce_fusion = (f32[1024]{0:T(1024)}, bf16[2308,1024]{1,0:T(8,128)(2,1)S(1)}, f32[2308,1024]{1,0:T(8,128)}) fusion(f32[2308,1024]{1,0:T(8,128)} %fusion.83, f32[1024]{0:T(1024)S(1)} %copy-done.34, bf16[2308,1024]{1,0:T(8,128)(2,1)} %all-gather.15.cloned.1.call-done, bf16[1024,1024]{1,0:T(8,128)(2,1)} %all-gather.13.cloned.1.call-done), kind=kOutput, calls=%fused_computation.62 | convolution fusion | flops 5017480192 | bytes 30466048 | tf_op jit(solution)/shard_map/dot_general | solution.py:22
  413.3 8.0 fusion.84
  421.8 13.0 multiply_convert_fusion.1
  434.8 10.0 convolution_convert_fusion
  444.9 54.5 %reduce-scatter.9.cloned.1.call-done = f32[2308,256]{1,0:T(8,128)} async-done(((f32[2308,1024]{1,0:T(8,128)}), f32[2308,256]{1,0:T(8,128)}) %reduce-scatter.9.cloned.1.call-update) | async-done | bytes 2363408 | tf_op jit(solution)/shard_map/reduce_scatter | solution.py:42
  503.6 11.4 all-reduce.1
  516.4 33.3 %reduce-scatter.7.cloned.1.call-done = bf16[2308,256]{1,0:T(8,128)(2,1)} async-done(((bf16[2308,1024]{1,0:T(8,128)(2,1)}), bf16[2308,256]{1,0:T(8,128)(2,1)}) %reduce-scatter.7.cloned.1.call-update) | async-done | bytes 1181712 | tf_op jit(solution)/shard_map/reduce_scatter | solution.py:161
  549.7 6.5 convert_reduce_fusion.5
  556.3 10.4 fusion.91
  566.8 8.9 fusion.92
  575.7 18.9 %all-gather.17.cloned.1.call-done = bf16[2308,1024]{1,0:T(8,128)(2,1)} async-done(((bf16[2308,256]{1,0:T(8,128)(2,1)}), bf16[2308,1024]{1,0:T(8,128)(2,1)}) %all-gather.17.cloned.1.call-update) | async-done | bytes 4726800 | tf_op jit(solution)/shard_map/all_gather | solution.py:38
  608.9 43.5 %while.27 = (s32[]{:T(128)}, bf16[4,577,4,64]{1,3,2,0:T(8,128)(2,1)}, bf16[4,577,4,64]{1,3,2,0:T(8,128)(2,1)}, bf16[4,577,4,64]{1,3,2,0:T(8,128)(2,1)}, bf16[4,5...) while((s32[]{:T(128)}, ...), condition=%wide.region_21.22_spmd, body=%wide.region_19.21_spmd.sunk | while | flops 869015040 | bytes 49986844 | solution.py:184
  672.3 5.4 fusion.90
  691.4 5.1 add_add_fusion
  696.9 415.2 %all-reduce.9.cloned.1.call-done = (f32[1024,256]{1,0:T(8,128)}, f32[1024,256]{1,0:T(8,128)}, f32[1024,256]{1,0:T(8,128)}, f32[256,1024]{1,0:T(8,128)}, f32[1024,1024]{1,0:T(8,128)}, /*index=5*/f32[1024,1024]{1,0:T(8,128)}) async-done(((f32[1024,256]{1,0:T(8,128)}, f32[1024,256]{1,0:T(8,128)}, f32[1024,256]{1,0:T(8,128)}, f32[256,1024]{1,0:T(8,128)}, f32[1024,1024]{1,0:T(8,128)}, ...) | async-done | bytes 12582928 | tf_op jit(solution)/shard_map/psum | solution.py:218
  1132.1 17.6 %psum.168 = f32[3072]{0:T(1024)} all-reduce(f32[3072]{0:T(1024)} %constant_dynamic-update-slice_fusion), channel_id=1, replica_groups=mesh['dp'=2,'row'=4,'col'=4] {'row'}, use_global_device_ids=true, to_apply=%region_42.43 | all-reduce | flops 3072 | bytes 24576 | tf_op jit(solution)/shard_map/psum | solution.py:218
  1149.7 10.1 psum.169
  1162.4 12.2 all-reduce
  1181.9 217.7 %all-reduce.11.cloned.1.call-done = (f32[1024,256]{1,0:T(8,128)}, f32[1024,256]{1,0:T(8,128)}, f32[1024,256]{1,0:T(8,128)}, f32[256,1024]{1,0:T(8,128)}, f32[1024,1024]{1,0:T(8,128)}, /*index=5*/f32[1024,1024]{1,0:T(8,128)}) async-done(((f32[1024,256]{1,0:T(8,128)}, f32[1024,256]{1,0:T(8,128)}, f32[1024,256]{1,0:T(8,128)}, f32[256,1024]{1,0:T(8,128)}, f32[1024,1024]{1,0:T(8,128)}, ...) | async-done | bytes 12582928 | tf_op jit(solution)/shard_map/psum | solution.py:217
  (231 shorter events, 214.9 us)
Async XLA Ops:
  8.0 19.1 %copy-start.27 = (bf16[256,256]{1,0:T(8,128)(2,1)S(1)}, bf16[256,256]{1,0:T(8,128)(2,1)}, u32[]{:S(2)}) copy-start(bf16[256,256]{1,0:T(8,128)(2,1)} %param.24) | copy-start | bytes 393220
  8.0 34.2 %copy-start.28 = (bf16[256,256]{1,0:T(8,128)(2,1)S(1)}, bf16[256,256]{1,0:T(8,128)(2,1)}, u32[]{:S(2)}) copy-start(bf16[256,256]{1,0:T(8,128)(2,1)} %param.22) | copy-start | bytes 393220
  8.0 51.6 %copy-start.29 = (bf16[256,256]{1,0:T(8,128)(2,1)S(1)}, bf16[256,256]{1,0:T(8,128)(2,1)}, u32[]{:S(2)}) copy-start(bf16[256,256]{1,0:T(8,128)(2,1)} %param.23) | copy-start | bytes 393220
  8.1 82.2 %all-gather.7.cloned.1.call-start = ((), (), s32[]{:S(2)}) async-start(), calls=%async_computation.4 | async-start | bytes 5918720 | tf_op jit(solution)/shard_map/all_gather | solution.py:34
  10.2 64.3 %copy-start.30 = (bf16[256,256]{1,0:T(8,128)(2,1)S(1)}, bf16[256,256]{1,0:T(8,128)(2,1)}, u32[]{:S(2)}) copy-start(bf16[256,256]{1,0:T(8,128)(2,1)} %param.27) | copy-start | bytes 393220
  23.9 66.4 %copy-start.36 = (f32[256]{0:T(256)S(1)}, f32[256]{0:T(256)}, u32[]{:S(2)}) copy-start(f32[256]{0:T(256)} %param.26) | copy-start | bytes 3076
  27.1 211.7 %reduce-scatter.5.cloned.1.call-start = ((), (), s32[]{:S(2)}) async-start(), calls=%async_computation.5 | async-start | bytes 11837440 | tf_op jit(solution)/shard_map/reduce_scatter | solution.py:151
  42.2 48.0 %copy-start.15 = (bf16[1024,256]{1,0:T(8,128)(2,1)}, bf16[1024,256]{1,0:T(8,128)(2,1)S(1)}, u32[]{:S(2)}) copy-start(bf16[1024,256]{1,0:T(8,128)(2,1)S(1)} %all_gather.31) | copy-start | bytes 1572868
  59.7 42.1 %copy-start.17 = (bf16[1024,256]{1,0:T(8,128)(2,1)}, bf16[1024,256]{1,0:T(8,128)(2,1)S(1)}, u32[]{:S(2)}) copy-start(bf16[1024,256]{1,0:T(8,128)(2,1)S(1)} %all_gather.32) | copy-start | bytes 1572868
  74.5 36.6 %copy-start.19 = (bf16[1024,256]{1,0:T(8,128)(2,1)}, bf16[1024,256]{1,0:T(8,128)(2,1)S(1)}, u32[]{:S(2)}) copy-start(bf16[1024,256]{1,0:T(8,128)(2,1)S(1)} %all_gather.33) | copy-start | bytes 1572868
  145.3 14.4 %copy-start.2 = (bf16[4,577,4,64]{1,3,2,0:T(8,128)(2,1)}, bf16[4,577,4,64]{1,3,2,0:T(8,128)(2,1)S(1)}, u32[]{:S(2)}) copy-start(bf16[4,577,4,64]{1,3,2,0:T(8,128)(2,1)S(1)} %get-tuple-element.416) | copy-start | bytes 3545092
  145.3 14.4 %copy-start.4 = (bf16[4,577,4,64]{1,3,2,0:T(8,128)(2,1)}, bf16[4,577,4,64]{1,3,2,0:T(8,128)(2,1)S(1)}, u32[]{:S(2)}) copy-start(bf16[4,577,4,64]{1,3,2,0:T(8,128)(2,1)S(1)} %get-tuple-element.417) | copy-start | bytes 3545092
  159.7 79.1 %copy-start = (bf16[2308,256]{1,0:T(8,128)(2,1)S(1)}, bf16[2308,256]{1,0:T(8,128)(2,1)}, u32[]{:S(2)}) copy-start(bf16[2308,256]{1,0:T(8,128)(2,1)} %param.21) | copy-start | bytes 3545092
  159.8 96.7 %all-gather.11.cloned.1.call-start = ((), (), s32[]{:S(2)}) async-start(), calls=%async_computation.7 | async-start | bytes 2621440 | tf_op jit(solution)/shard_map/all_gather | solution.py:137
  160.3 91.9 %copy-start.32 = (f32[256]{0:T(256)S(1)}, f32[256]{0:T(256)}, u32[]{:S(2)}) copy-start(f32[256]{0:T(256)} %param.35) | copy-start | bytes 3076
  160.3 133.4 %all-gather.9.cloned.1.call-start = ((), (), s32[]{:S(2)}) async-start(), calls=%async_computation.6 | async-start | bytes 5918720 | tf_op jit(solution)/shard_map/all_gather | solution.py:34
  255.0 86.3 %all-gather.13.cloned.1.call-start = ((), (), s32[]{:S(2)}) async-start(), calls=%async_computation.8 | async-start | bytes 2621440 | tf_op jit(solution)/shard_map/all_gather | solution.py:138
  255.6 123.5 %all-gather.15.cloned.1.call-start = ((), (), s32[]{:S(2)}) async-start(), calls=%async_computation.10 | async-start | bytes 5918720 | tf_op jit(solution)/shard_map/all_gather | solution.py:38
  256.4 122.8 %copy-start.34 = (f32[1024]{0:T(1024)S(1)}, f32[1024]{0:T(1024)}, u32[]{:S(2)}) copy-start(f32[1024]{0:T(1024)} %param.30) | copy-start | bytes 12292
  256.4 243.0 %reduce-scatter.9.cloned.1.call-start = ((), (), s32[]{:S(2)}) async-start(), calls=%async_computation.11 | async-start | bytes 11837440 | tf_op jit(solution)/shard_map/reduce_scatter | solution.py:42
  379.1 34.2 %copy-start.35 = (bf16[1024,1024]{1,0:T(8,128)(2,1)S(1)}, bf16[1024,1024]{1,0:T(8,128)(2,1)}, u32[]{:S(2)}) copy-start(bf16[1024,1024]{1,0:T(8,128)(2,1)} %all-gather.11.cloned.1.call-done) | copy-start | bytes 6291460
  421.4 128.4 %reduce-scatter.7.cloned.1.call-start = ((), (), s32[]{:S(2)}) async-start(), calls=%async_computation.9 | async-start | bytes 5918720 | tf_op jit(solution)/shard_map/reduce_scatter | solution.py:161
  444.8 104.9 %copy-start.14 = (bf16[2308,256]{1,0:T(8,128)(2,1)S(1)}, bf16[2308,256]{1,0:T(8,128)(2,1)}, u32[]{:S(2)}) copy-start(bf16[2308,256]{1,0:T(8,128)(2,1)} %param.37) | copy-start | bytes 3545092
  444.8 149.7 %all-gather.17.cloned.1.call-start = ((), (), s32[]{:S(2)}) async-start(), calls=%async_computation.12 | async-start | bytes 5918720 | tf_op jit(solution)/shard_map/all_gather | solution.py:38
  556.2 10.5 slice-start
  556.3 555.8 %all-reduce.9.cloned.1.call-start = ((), (), s32[]{:S(2)}) async-start(), calls=%async_computation.14 | async-start | bytes 25165824 | tf_op jit(solution)/shard_map/psum | solution.py:218
  566.8 27.8 %copy-start.22 = (bf16[256,1024]{1,0:T(8,128)(2,1)S(1)}, bf16[256,1024]{1,0:T(8,128)(2,1)}, u32[]{:S(2)}) copy-start(bf16[256,1024]{1,0:T(8,128)(2,1)} %all_gather.34) | copy-start | bytes 1572868
  665.1 12.6 slice-start.2
  685.9 436.7 %reduce-scatter.11.cloned.1.call-start = ((), (), s32[]{:S(2)}) async-start(), calls=%async_computation.13 | async-start | bytes 11837440 | tf_op jit(solution)/shard_map/reduce_scatter | solution.py:42
  696.6 703.0 %all-reduce.11.cloned.1.call-start = ((), (), s32[]{:S(2)}) async-start(), calls=%async_computation.15 | async-start | bytes 25165824 | tf_op jit(solution)/shard_map/psum | solution.py:217
  1112.0 10.5 copy-start.31
  1114.5 62.2 %copy-start.8 = (f32[2308,256]{1,0:T(8,128)S(1)}, f32[2308,256]{1,0:T(8,128)}, u32[]{:S(2)}) copy-start(f32[2308,256]{1,0:T(8,128)} %get-tuple-element.205) | copy-start | bytes 7090180
  (26 other events, 107.2 us)
Sparse Core Ops, SparseCore 0:
  27.2 38.4 all-gather.6
  159.9 78.8 reduce-scatter.4
  556.4 38.1 all-gather.16
  696.7 78.0 reduce-scatter.10
  1112.2 287.3 all-reduce.10
Sparse Core Ops, SparseCore 1:
  161.8 46.4 all-gather.10
  255.1 38.5 all-gather.8
  295.2 46.1 all-gather.12
  342.9 36.2 all-gather.14
  421.4 77.8 reduce-scatter.8
  501.9 47.8 reduce-scatter.6
  686.0 426.0 all-reduce.8
